TPU v7x, 256 devices: a whole 4x4x8 slice. The times are simulated.
256 devices in a mesh: ctx: 8 (over x, y_hi), mp: 32 (over z, y_lo, core).
Axes of the slice: x: 4, y: 4 (y_hi: 2, y_lo: 2; y = y_hi * 2 + y_lo), z: 8, core: 2. Of those that a mesh axis runs over, the one named last changes fastest.
Arguments:
- activations: bfloat16 [8192, 4096], P('ctx', 'mp'), may hold values from -36 to 36
- norm_gain: float32 [4096], P('mp'), may hold values from 0.1 to 1.9
- w_in: bfloat16 [4096, 3, 4096], P('ctx', None, 'mp'), may hold values from -0.09375 to 0.09375
- tail_rows: bfloat16 [3, 4096, 2], P(None, 'mp'), may hold values from -4 to 4
- short_filter: float32 [3, 3, 4096], P(None, None, 'mp'), may hold values from -3 to 3
- decay_rate: float32 [4096, 16], P('mp'), may hold values from 2.4414063e-05 to 0.08, as said below
- residue: float32 [4096, 16], P('mp'), may hold values from -1.5 to 1.5
- skip_gain: float32 [4096], P('mp'), may hold values from -4 to 4
- state_in: float32 [4096, 16], P('mp'), may hold values from -4 to 4
- w_out: bfloat16 [4096, 4096], P('mp', 'ctx'), may hold values from -0.1875 to 0.1875
Outputs:
- block_out: bfloat16 [8192, 4096], P('ctx', 'mp')
- state_out: float32 [4096, 16], P('mp')
Inputs may be any that keep to these rules, and one draw needn't show every extreme that they name: `decay_rate`: every rate lies between 0.2/8192 and 0.08; any share of the modes may be slow (below 2/8192) or fast.
All inputs are finite; a program needn't handle non-finite values.
Results may differ from a plain program's by a relative error of at most 0.03.
Values may be sent and summed in bfloat16 or wider, within the bound.
A program may use at most 64 MiB of HBM per device.

v0:
```python
import math
import jax
import jax.numpy as jnp
import numpy as np
from jax import lax
from jax.sharding import PartitionSpec as P

highest = lax.Precision.HIGHEST


def from_behind(block, axis, distance):
    devices = range(lax.axis_size(axis))
    route = [(i - distance, i) for i in devices if i - distance in devices]
    return lax.ppermute(block, axis, route)


def pick_rows(array_in, offset, share):
    return lax.dynamic_slice_in_dim(array_in, offset, share, 0)


def chain_step(first, second):
    return (first[0] * second[0], second[0] * first[1] + second[1])


def block_powers(rate_rows, block_size):
    steps_in = jnp.arange(block_size, dtype=jnp.float32)
    return jnp.exp(-rate_rows[:, :, None] * steps_in[None, None, :])


def carried_response(entering, rate_rows, residues, block_size):
    powers = block_powers(rate_rows, block_size)
    lifted = residues[:, :, None] * jnp.exp(-rate_rows)[:, :, None] * powers
    return jnp.einsum("ckn,cnt->ckt", entering, lifted, precision=highest)


def initial_response(initial, rate_rows, residues, length):
    block_size = math.gcd(64, length)
    blocks = length // block_size
    index_k = jnp.arange(blocks, dtype=jnp.float32) * block_size
    carried = jnp.exp(-rate_rows[:, None, :] * index_k[None, :, None]) * initial[:, None, :]
    return carried_response(carried, rate_rows, residues, block_size).reshape(
        initial.shape[0], length
    )


def modal_conv(signal, rate_rows, residues, skip_rows, initial):
    channels, length = signal.shape
    block_size = math.gcd(64, length)
    blocks = length // block_size
    values = signal.astype(jnp.float32)
    shaped = values.reshape(channels, blocks, block_size)
    powers = block_powers(rate_rows, block_size)
    scales = jnp.sqrt(-jnp.expm1(-2.0 * rate_rows))
    kernel = jnp.einsum("cn,cnb->cb", residues * scales, powers, precision=highest)
    offsets = np.arange(block_size)[:, None] - np.arange(block_size)[None, :]
    clipped = np.clip(offsets, 0, block_size - 1)
    toeplitz = jnp.where(offsets[None] >= 0, kernel[:, clipped], 0.0)
    within = jnp.einsum("cts,cks->ckt", toeplitz, shaped, precision=highest)
    loading = jnp.einsum(
        "cks,cns->ckn", shaped, scales[:, :, None] * powers[:, :, ::-1], precision=highest
    )
    decays = jnp.broadcast_to(jnp.exp(-rate_rows * block_size)[:, None, :], loading.shape)
    decay_all, block_ends = lax.associative_scan(chain_step, (decays, loading), axis=1)
    entering = jnp.concatenate([jnp.zeros_like(block_ends[:, :1]), block_ends[:, :-1]], axis=1)
    response = (within + carried_response(entering, rate_rows, residues, block_size)).reshape(
        channels, length
    )
    response = response + initial_response(initial, rate_rows, residues, length)
    final = block_ends[:, -1] + jnp.exp(-rate_rows * length) * initial
    return (response + skip_rows[:, None] * values, final)


def local(
    activations,
    norm_gain,
    w_in,
    tail_rows,
    short_filter,
    decay_rate,
    residue,
    skip_gain,
    state_in,
    w_out,
):
    tok_rows, feature_width = activations.shape
    model_width = feature_width * lax.axis_size("mp")
    act_float = activations.astype(jnp.float32)
    squares = lax.psum(jnp.sum(act_float * act_float, axis=1), "mp")
    inverse = lax.rsqrt(squares / model_width + 1e-06)
    normed = (act_float * inverse[:, None] * norm_gain[None, :]).astype(jnp.bfloat16)
    panel = lax.all_gather(w_in, "ctx", axis=0, tiled=True).reshape(model_width, 3 * feature_width)
    proj_sum = lax.dot_general(
        panel,
        lax.all_gather(normed, "mp", axis=1, tiled=True),
        (((0,), (1,)), ((), ())),
        preferred_element_type=jnp.float32,
    )
    projected = proj_sum.astype(jnp.bfloat16).reshape(3, feature_width, tok_rows)
    incoming = from_behind(projected[:, :, -2:], "ctx", 1)
    incoming = jnp.where(lax.axis_index("ctx") == 0, tail_rows, incoming)
    extended = jnp.concatenate([incoming, projected], axis=2).astype(jnp.float32)
    smoothed = short_filter[0][:, :, None] * extended[:, :, 2:]
    smoothed = smoothed + short_filter[1][:, :, None] * extended[:, :, 1:-1]
    smoothed = smoothed + short_filter[2][:, :, None] * extended[:, :, :-2]
    query = smoothed[0]
    mixed = (smoothed[1] * smoothed[2]).astype(jnp.bfloat16)
    share = feature_width // lax.axis_size("ctx")
    offset = lax.axis_index("ctx") * share
    whole = lax.all_to_all(mixed, "ctx", split_axis=0, concat_axis=1, tiled=True)
    filtered, final_part = modal_conv(
        whole,
        pick_rows(decay_rate, offset, share),
        pick_rows(residue, offset, share),
        pick_rows(skip_gain, offset, share),
        pick_rows(state_in, offset, share),
    )
    response = lax.all_to_all(filtered, "ctx", split_axis=1, concat_axis=0, tiled=True)
    final_state = lax.all_gather(final_part, "ctx", axis=0, tiled=True)
    gated = (query * response).astype(jnp.bfloat16)
    out_panel = lax.all_gather(w_out, "ctx", axis=1, tiled=True)
    branch = (
        lax.psum_scatter(
            lax.dot_general(
                out_panel, gated, (((0,), (0,)), ((), ())), preferred_element_type=jnp.float32
            ).astype(jnp.bfloat16),
            "mp",
            scatter_dimension=0,
            tiled=True,
        )
        .astype(jnp.float32)
        .T
    )
    return ((act_float + branch).astype(jnp.bfloat16), final_state)


def solution(mesh):
    placed = (
        P("ctx", "mp"),
        P("mp"),
        P("ctx", None, "mp"),
        P(None, "mp", None),
        P(None, None, "mp"),
        P("mp", None),
        P("mp", None),
        P("mp"),
        P("mp", None),
        P("mp", "ctx"),
    )
    return jax.shard_map(
        local,
        mesh=mesh,
        in_specs=placed,
        out_specs=(P("ctx", "mp"), P("mp", None)),
        check_vma=False,
    )
```

profile of v0, /device:TPU:4, one launch (start us, length us, event | category | flops | bytes accessed | tf_op | source)
XLA Modules:
  0.0 457.9 jit_solution(16043692956074559367)
XLA Ops:
  7.3 1.9 copy.85
  9.3 1.2 fusion.2
  10.4 59.9 %psum.7 = f32[1024]{0:T(1024)S(1)} all-reduce(f32[1024]{0:T(1024)S(1)} %fusion.2), channel_id=1, replica_groups=mesh['ctx'=8,'mp'=32] {'mp'}, use_global_device_ids=true, to_apply=%region_1.0 | all-reduce | flops 1024 | bytes 8192 | tf_op jit(solution)/shard_map/psum | solution.py:88
  70.4 1.9 fusion.4
  73.9 11.3 %all-gather.6.cloned.1.call-done = bf16[4096,3,128]{0,2,1:T(8,128)(2,1)} async-done(((bf16[512,3,128]{0,2,1:T(8,128)(2,1)}), bf16[4096,3,128]{0,2,1:T(8,128)(2,1)}) %all-gather.6.cloned.1.call-update) | async-done | bytes 3145744 | tf_op jit(solution)/shard_map/all_gather | solution.py:91
  85.3 92.4 %all-gather.4.cloned.1.call-done = bf16[1024,4096]{1,0:T(8,128)(2,1)} async-done(((bf16[1024,128]{1,0:T(8,128)(2,1)}), bf16[1024,4096]{1,0:T(8,128)(2,1)}) %all-gather.4.cloned.1.call-update) | async-done | bytes 8388624 | tf_op jit(solution)/shard_map/all_gather | solution.py:94
  177.6 7.7 %convolution_convert_fusion = bf16[1024,384]{0,1:T(8,128)(2,1)S(1)} fusion(bf16[1024,4096]{1,0:T(8,128)(2,1)} %all-gather.4.cloned.1.call-done, bf16[4096,384]{0,1:T(8,128)(2,1)} %bitcast.65), kind=kOutput, calls=%fused_computation.7 | convolution fusion | flops 3221618688 | bytes 12320768 | tf_op jit(solution)/shard_map/dot_general | solution.py:92
  185.5 3.9 collective-permute-start
  189.7 5.1 %collective-permute-done = bf16[3,128,2]{2,1,0:T(8,128)(2,1)S(1)} collective-permute-done((bf16[3,128,2]{2,1,0:T(8,128)(2,1)S(1)}, bf16[3,128,2]{2,1,0:T(8,128)(2,1)S(1)}, u32[]{:S(2)}, u32[]{:S(2)}) %collective-permute-start) | collective-permute-done | bytes 1568 | tf_op jit(solution)/shard_map/ppermute | solution.py:14
  195.2 1.2 fusion
  197.2 6.7 %all-to-all-start = ((bf16[8,16,1024]{2,1,0:T(8,128)(2,1)}), bf16[8,16,1024]{2,1,0:T(8,128)(2,1)S(1)}, u32[]{:S(2)}, u32[]{:S(2)}) async-start(bf16[8,16,1024]{2,1,0:T(8,128)(2,1)} %bitcast.7), calls=%async_computation | async-start | bytes 524288 | tf_op jit(solution)/shard_map/all_to_all | solution.py:109
  207.4 2.8 all-to-all-done
  211.7 2.9 slice.235
  214.6 2.3 slice.195
  217.0 2.3 slice.194
  219.4 1.9 slice.233
  221.3 1.3 slice.200
  222.5 1.2 slice.199
  223.9 1.3 slice.231
  226.8 1.0 slice.229
  231.7 1.0 multiply_add_fusion.1
  233.8 1.0 multiply_add_fusion
  235.8 6.2 %pad.47 = f32[16,4,16]{1,2,0:T(8,128)S(1)} pad(f32[16,2,16]{1,2,0:T(8,128)} %pad_add_fusion, f32[]{:T(128)} %constant.7.clone.1), padding=0_0_0x1_0_1x0_0_0 | pad | bytes 6148 | tf_op jit(solution)/shard_map/pad | solution.py:63
  242.1 1.1 pad.46
  243.3 1.0 fusion.18
  244.5 1.2 pad.48
  245.7 1.2 pad.49
  246.9 1.0 fusion.17
  248.1 1.3 pad.50
  249.4 1.4 pad.51
  251.8 1.6 pad.52
  253.4 1.6 pad.53
  256.0 2.1 pad.54
  258.1 2.2 pad.55
  260.3 3.2 pad.95
  263.5 3.2 pad.57
  267.0 3.2 pad.56
  270.9 14.2 %gather_fusion = f32[4096,16]{1,0:T(8,128)} fusion(f32[16,64]{0,1:T(8,128)S(1)} %bitcast.53, s32[4096]{0:T(1024)S(1)} %copy-done.5), kind=kCustom, calls=%fused_computation | custom fusion | bytes 540672 | tf_op jit(solution)/shard_map/gather | solution.py:57
  285.1 2.3 copy.90
  287.4 1.1 fusion.9
  288.5 1.1 convolution_add_fusion.1
  289.7 1.2 convolution_add_fusion
  291.9 12.7 %all_to_all.29 = f32[16,8,1024]{2,0,1:T(8,128)S(1)} all-to-all(f32[16,8,1024]{2,0,1:T(8,128)S(1)} %copy_add_fusion), channel_id=1, replica_groups=mesh['ctx'=8,'mp'=32] {'ctx'}, dimensions={1} | all-to-all | bytes 1048576 | tf_op jit(solution)/shard_map/all_to_all | solution.py:117
  304.7 6.9 %convert_bitcast_fusion = bf16[4096,1024]{0,1:T(8,128)(2,1)} fusion(bf16[128,1024]{1,0:T(8,128)(2,1)S(1)} %fusion.8, bf16[128,4096]{1,0:T(8,128)(2,1)} %all-gather.8.cloned.1.call-done), kind=kOutput, calls=%fused_computation.1 | convolution fusion | flops 1077936128 | bytes 9699328 | tf_op jit(solution)/shard_map/dot_general | solution.py:123
  311.6 11.9 %copy.103 = bf16[4096,1024]{1,0:T(8,128)(2,1)} copy(bf16[4096,1024]{0,1:T(8,128)(2,1)} %convert_bitcast_fusion) | data formatting | bytes 16777216
  323.5 32.6 %all_gather.15 = f32[128,16]{1,0:T(8,128)S(1)} all-gather(f32[16,16]{1,0:T(8,128)S(1)} %get-tuple-element.20), channel_id=1, replica_groups=mesh['ctx'=8,'mp'=32] {'ctx'}, dimensions={0}, use_global_device_ids=true | all-gather | bytes 9216 | tf_op jit(solution)/shard_map/all_gather | solution.py:118
  356.8 92.7 %reduce-scatter.4.cloned.1.call-done = bf16[128,1024]{1,0:T(8,128)(2,1)} async-done(((bf16[4096,1024]{1,0:T(8,128)(2,1)}), bf16[128,1024]{1,0:T(8,128)(2,1)}) %reduce-scatter.4.cloned.1.call-update) | async-done | bytes 262160
  449.5 1.1 copy.104
  (119 shorter events, 21.5 us)
Async XLA Ops:
  7.2 182.2 %copy-start = (f32[128,16]{0,1:T(8,128)S(1)}, f32[128,16]{0,1:T(8,128)}, u32[]{:S(2)}) copy-start(f32[128,16]{0,1:T(8,128)} %param.19) | copy-start | bytes 24580
  7.2 65.8 %copy-start.18 = (f32[3,3,128]{2,1,0:T(4,128)S(1)}, f32[3,3,128]{2,1,0:T(4,128)}, u32[]{:S(2)}) copy-start(f32[3,3,128]{2,1,0:T(4,128)} %param.17) | copy-start | bytes 13828
  7.2 65.8 %copy-start.16 = (f32[128,16]{0,1:T(8,128)S(1)}, f32[128,16]{0,1:T(8,128)}, u32[]{:S(2)}) copy-start(f32[128,16]{0,1:T(8,128)} %param.21) | copy-start | bytes 24580
  7.2 65.8 %copy-start.17 = (f32[128,16]{0,1:T(8,128)S(1)}, f32[128,16]{0,1:T(8,128)}, u32[]{:S(2)}) copy-start(f32[128,16]{0,1:T(8,128)} %param.18) | copy-start | bytes 24580
  7.2 78.0 %all-gather.6.cloned.1.call-start = ((), (), s32[]{:S(2)}) async-start(), calls=%async_computation.4 | async-start | bytes 3538944 | tf_op jit(solution)/shard_map/all_gather | solution.py:91
  9.2 168.4 %all-gather.4.cloned.1.call-start = ((), (), s32[]{:S(2)}) async-start(), calls=%async_computation.3 | async-start | bytes 8650752 | tf_op jit(solution)/shard_map/all_gather | solution.py:94
  72.2 232.5 %all-gather.8.cloned.1.call-start = ((), (), s32[]{:S(2)}) async-start(), calls=%async_computation.5 | async-start | bytes 1179648 | tf_op jit(solution)/shard_map/all_gather | solution.py:120
  73.2 112.2 %copy-start.11 = (f32[16,16]{1,0:T(8,128)}, f32[16,16]{1,0:T(8,128)S(1)}, u32[]{:S(2)}) copy-start(f32[16,16]{1,0:T(8,128)S(1)} %copy.106) | copy-start | bytes 3076
  73.8 145.5 %copy-start.7 = (f32[16,16]{1,0:T(8,128)}, f32[16,16]{1,0:T(8,128)S(1)}, u32[]{:S(2)}) copy-start(f32[16,16]{1,0:T(8,128)S(1)} %get-tuple-element.27) | copy-start | bytes 3076
  73.8 150.0 %copy-start.9 = (f32[16,16]{1,0:T(8,128)}, f32[16,16]{1,0:T(8,128)S(1)}, u32[]{:S(2)}) copy-start(f32[16,16]{1,0:T(8,128)S(1)} %get-tuple-element.28) | copy-start | bytes 3076
  73.8 152.8 %copy-start.10 = (f32[16,16]{1,0:T(8,128)}, f32[16,16]{1,0:T(8,128)S(1)}, u32[]{:S(2)}) copy-start(f32[16,16]{1,0:T(8,128)S(1)} %get-tuple-element.22) | copy-start | bytes 3076
  177.6 11.9 %copy-start.19 = (bf16[3,128,2]{1,2,0:T(2,128)(2,1)S(1)}, bf16[3,128,2]{1,2,0:T(2,128)(2,1)}, u32[]{:S(2)}) copy-start(bf16[3,128,2]{1,2,0:T(2,128)(2,1)} %param.16) | copy-start | bytes 4612
  185.5 9.4 %collective-permute-start = (bf16[3,128,2]{2,1,0:T(8,128)(2,1)S(1)}, bf16[3,128,2]{2,1,0:T(8,128)(2,1)S(1)}, u32[]{:S(2)}, u32[]{:S(2)}) collective-permute-start(bf16[3,128,2]{2,1,0:T(8,128)(2,1)S(1)} %slice.240), channel_id=1, source_target_pairs={{0,32},{32,64},{64,96},{96,128},{128,160},{160,192},{192,224},{1,3... | collective-permute-start | bytes 4616 | tf_op jit(solution)/shard_map/ppermute | solution.py:14
  196.4 8.0 %copy-start.22 = (f32[128]{0:T(128)S(1)}, f32[128]{0:T(128)}, u32[]{:S(2)}) copy-start(f32[128]{0:T(128)} %param.20) | copy-start | bytes 1540
  196.4 10.4 %copy-start.14 = (s32[4096]{0:T(1024)S(1)}, s32[4096]{0:T(1024)}, u32[]{:S(2)}) copy-start(s32[4096]{0:T(1024)} %constant.70) | copy-start | bytes 49156
  197.2 13.0 %all-to-all-start = ((bf16[8,16,1024]{2,1,0:T(8,128)(2,1)}), bf16[8,16,1024]{2,1,0:T(8,128)(2,1)S(1)}, u32[]{:S(2)}, u32[]{:S(2)}) async-start(bf16[8,16,1024]{2,1,0:T(8,128)(2,1)} %bitcast.7), calls=%async_computation | async-start | bytes 524288 | tf_op jit(solution)/shard_map/all_to_all | solution.py:109
  203.9 245.6 %reduce-scatter.4.cloned.1.call-start = ((), (), s32[]{:S(2)}) async-start(), calls=%async_computation.6 | async-start | bytes 8650752
  243.3 7.5 %copy-start.4 = (f32[16,15,16]{1,2,0:T(8,128)S(1)}, f32[16,15,16]{1,2,0:T(8,128)}, u32[]{:S(2)}) copy-start(f32[16,15,16]{1,2,0:T(8,128)} %slice.231) | copy-start | bytes 46084
  246.9 8.1 %copy-start.3 = (f32[16,31,16]{1,2,0:T(8,128)S(1)}, f32[16,31,16]{1,2,0:T(8,128)}, u32[]{:S(2)}) copy-start(f32[16,31,16]{1,2,0:T(8,128)} %slice.233) | copy-start | bytes 95236
  251.6 15.1 %copy-start.2 = (f32[16,63,16]{1,2,0:T(8,128)S(1)}, f32[16,63,16]{1,2,0:T(8,128)}, u32[]{:S(2)}) copy-start(f32[16,63,16]{1,2,0:T(8,128)} %slice.235) | copy-start | bytes 193540
  251.6 15.1 %copy-start.8 = (f32[16,16]{1,0:T(8,128)S(1)}, f32[16,16]{1,0:T(8,128)}, u32[]{:S(2)}) copy-start(f32[16,16]{1,0:T(8,128)} %copy-done.7) | copy-start | bytes 3076
  255.8 14.6 %copy-start.6 = (f32[16,16]{1,0:T(8,128)S(1)}, f32[16,16]{1,0:T(8,128)}, u32[]{:S(2)}) copy-start(f32[16,16]{1,0:T(8,128)} %copy.107) | copy-start | bytes 3076
  255.8 14.6 %copy-start.12 = (f32[16,16]{1,0:T(8,128)S(1)}, f32[16,16]{1,0:T(8,128)}, u32[]{:S(2)}) copy-start(f32[16,16]{1,0:T(8,128)} %copy-done.11) | copy-start | bytes 3076
  255.8 14.6 %copy-start.13 = (f32[16,16]{1,0:T(8,128)S(1)}, f32[16,16]{1,0:T(8,128)}, u32[]{:S(2)}) copy-start(f32[16,16]{1,0:T(8,128)} %copy.105) | copy-start | bytes 3076
  256.0 14.9 %copy-start.5 = (s32[4096]{0:T(1024)S(1)}, s32[4096]{0:T(1024)}, u32[]{:S(2)}) copy-start(s32[4096]{0:T(1024)} %broadcast_clamp_fusion) | copy-start | bytes 49156
  285.1 2.3 copy-start.15
  287.4 2.3 copy-start.21
  290.9 0.7 copy-start.20
  323.5 127.2 %copy-start.1 = (bf16[1024,128]{1,0:T(8,128)(2,1)S(1)}, bf16[1024,128]{1,0:T(8,128)(2,1)}, u32[]{:S(2)}) copy-start(bf16[1024,128]{1,0:T(8,128)(2,1)} %param.13) | copy-start | bytes 786436
Sparse Core Ops, SparseCore 0:
  10.5 74.6 all-gather.5
  87.6 89.9 all-gather.3
  180.1 49.9 all-gather.7
  323.6 125.8 reduce-scatter.3
where the time goes:
time: 459 us; the launch traced here: 458 us
  waiting for transfers between devices  205 us (45%)
  blocking collectives  105 us (23%)
  local copies, waits for them, and re-layouts  85.8 us (19%)
  matrix products  19.3 us (4%)
  other arithmetic  17.2 us (4%)
  between operations  14.5 us (3%)
  starting transfers between devices  10.7 us (2%)
    unnamed x5, waiting for transfers between devices  93.4 us
    all_gather x1, waiting for transfers between devices, local(): lax.all_gather(normed, 'mp', axis=1, tiled=True)  92.4 us
    psum x1, blocking collectives, local(): squares = lax.psum(jnp.sum(act_float * act_float, axis=1), 'mp')  59.9 us
    all_gather x1, blocking collectives, local(): final_state = lax.all_gather(final_part, 'ctx', axis=0, tiled=True)  32.6 us
    pad x12, local copies, waits for them, and re-layouts, modal_conv(): lax.associative_scan(chain_step, (decays, loading), axis=1)  26.4 us
    unnamed x55, local copies, waits for them, and re-layouts  20.5 us
    slice x19, local copies, waits for them, and re-layouts, modal_conv(): lax.associative_scan(chain_step, (decays, loading), axis=1)  20.2 us
    gather x2, local copies, waits for them, and re-layouts, modal_conv(): toeplitz = jnp.where(offsets[None] >= 0, kernel[:, clipped], 0.0)  16.5 us
  transfers between devices with their start and end apart: 6, of which 5 were waited for; matrix products, arithmetic and copies ran while one was open for 22% of the time, Pallas kernels for 0%

commit v1 on v0

--- a/solution.py
+++ b/solution.py
@@ -85,7 +85,7 @@
     tok_rows, feature_width = activations.shape
     model_width = feature_width * lax.axis_size("mp")
     act_float = activations.astype(jnp.float32)
-    squares = lax.psum(jnp.sum(act_float * act_float, axis=1), "mp")
+    squares = jnp.sum(lax.all_gather(jnp.sum(act_float * act_float, axis=1), "mp"), axis=0)
     inverse = lax.rsqrt(squares / model_width + 1e-06)
     normed = (act_float * inverse[:, None] * norm_gain[None, :]).astype(jnp.bfloat16)
     panel = lax.all_gather(w_in, "ctx", axis=0, tiled=True).reshape(model_width, 3 * feature_width)

time: 459 us -> 483 us (1.052)
  waiting for transfers between devices: 205 us -> 228 us
  blocking collectives: 105 us -> 82.9 us
  local copies, waits for them, and re-layouts: 85.8 us -> 101 us
  other arithmetic: 17.2 us -> 24 us
    psum x1 -> x0, blocking collectives: 59.9 us -> none  [local(): squares = lax.psum(jnp.sum(act_float * act_float, axis=1), 'mp')]
    all_gather x0 -> x1, blocking collectives: none -> 37.7 us  [local(): lax.all_gather(jnp.sum(act_float * act_float, axis=1), 'mp')]
    all_gather x1, waiting for transfers between devices: 11.3 us -> 33.9 us  [local(): lax.all_gather(w_in, 'ctx', axis=0, tiled=True)]
    pad x12, local copies, waits for them, and re-layouts: 26.4 us -> 36.5 us  [modal_conv(): lax.associative_scan(chain_step, (decays, loading), axis=1)]
    unnamed x55 -> x43, local copies, waits for them, and re-layouts: 20.5 us -> 20.2 us
  transfers between devices with their start and end apart: 6 -> 6, of which waited for: 5 -> 5; matrix products, arithmetic and copies ran while one was open for 22% -> 26% of each run, Pallas kernels for 0% -> 0%
where the time goes in v1:
time: 483 us; the launch traced here: 481 us
  waiting for transfers between devices  228 us (47%)
  local copies, waits for them, and re-layouts  101 us (21%)
  blocking collectives  82.9 us (17%)
  other arithmetic  24 us (5%)
  matrix products  20.1 us (4%)
  between operations  14.4 us (3%)
  starting transfers between devices  10.7 us (2%)
    unnamed x5, waiting for transfers between devices  93.9 us
    all_gather x1, waiting for transfers between devices, local(): lax.all_gather(normed, 'mp', axis=1, tiled=True)  92.6 us
    all_gather x1, blocking collectives, local(): lax.all_gather(jnp.sum(act_float * act_float, axis=1), 'mp')  37.7 us
    pad x12, local copies, waits for them, and re-layouts, modal_conv(): lax.associative_scan(chain_step, (decays, loading), axis=1)  36.5 us
    all_gather x1, waiting for transfers between devices, local(): lax.all_gather(w_in, 'ctx', axis=0, tiled=True)  33.9 us
    all_gather x1, blocking collectives, local(): final_state = lax.all_gather(final_part, 'ctx', axis=0, tiled=True)  32.5 us
    slice x19, local copies, waits for them, and re-layouts, modal_conv(): lax.associative_scan(chain_step, (decays, loading), axis=1)  22.6 us
    unnamed x43, local copies, waits for them, and re-layouts  20.2 us
  transfers between devices with their start and end apart: 6, of which 5 were waited for; matrix products, arithmetic and copies ran while one was open for 26% of the time, Pallas kernels for 0%

profile of v1, /device:TPU:4, one launch (start us, length us, event | category | flops | bytes accessed | tf_op | source)
XLA Modules:
  0.0 480.9 jit_solution(4780699343409475472)
XLA Ops:
  7.3 2.0 copy.85
  9.4 1.2 fusion.2
  10.5 37.7 %all-gather = f32[32768]{0:T(1024)S(1)} all-gather(f32[1024]{0:T(1024)S(1)} %fusion.2), channel_id=2, replica_groups=mesh['ctx'=8,'mp'=32] {'mp'}, dimensions={0}, use_global_device_ids=true | all-gather | bytes 135168 | tf_op jit(solution)/shard_map/all_gather | solution.py:88
  50.9 33.9 %all-gather.7.cloned.1.call-done = bf16[4096,3,128]{0,2,1:T(8,128)(2,1)} async-done(((bf16[512,3,128]{0,2,1:T(8,128)(2,1)}), bf16[4096,3,128]{0,2,1:T(8,128)(2,1)}) %all-gather.7.cloned.1.call-update) | async-done | bytes 3145744 | tf_op jit(solution)/shard_map/all_gather | solution.py:91
  84.8 92.6 %all-gather.5.cloned.1.call-done = bf16[1024,4096]{1,0:T(8,128)(2,1)} async-done(((bf16[1024,128]{1,0:T(8,128)(2,1)}), bf16[1024,4096]{1,0:T(8,128)(2,1)}) %all-gather.5.cloned.1.call-update) | async-done | bytes 8388624 | tf_op jit(solution)/shard_map/all_gather | solution.py:94
  177.4 7.7 %convolution_convert_fusion = bf16[1024,384]{0,1:T(8,128)(2,1)S(1)} fusion(bf16[1024,4096]{1,0:T(8,128)(2,1)} %all-gather.5.cloned.1.call-done, bf16[4096,384]{0,1:T(8,128)(2,1)} %bitcast.65), kind=kOutput, calls=%fused_computation.7 | convolution fusion | flops 3221618688 | bytes 12320768 | tf_op jit(solution)/shard_map/dot_general | solution.py:92
  185.2 4.0 collective-permute-start
  189.4 5.1 %collective-permute-done = bf16[3,128,2]{2,1,0:T(8,128)(2,1)S(1)} collective-permute-done((bf16[3,128,2]{2,1,0:T(8,128)(2,1)S(1)}, bf16[3,128,2]{2,1,0:T(8,128)(2,1)S(1)}, u32[]{:S(2)}, u32[]{:S(2)}) %collective-permute-start) | collective-permute-done | bytes 1568 | tf_op jit(solution)/shard_map/ppermute | solution.py:14
  195.0 1.2 fusion
  197.0 6.7 %all-to-all-start = ((bf16[8,16,1024]{2,1,0:T(8,128)(2,1)}), bf16[8,16,1024]{2,1,0:T(8,128)(2,1)S(1)}, u32[]{:S(2)}, u32[]{:S(2)}) async-start(bf16[8,16,1024]{2,1,0:T(8,128)(2,1)} %bitcast.7), calls=%async_computation | async-start | bytes 524288 | tf_op jit(solution)/shard_map/all_to_all | solution.py:109
  207.9 2.1 all-to-all-done
  211.5 2.9 slice.235
  214.4 2.3 slice.195
  216.7 2.3 slice.194
  219.2 1.9 slice.233
  221.0 1.3 slice.200
  222.3 1.2 slice.199
  223.7 1.3 slice.231
  233.4 1.1 multiply_add_fusion.1
  238.1 1.7 fusion.44
  239.8 6.2 %pad.47 = f32[16,4,16]{1,2,0:T(8,128)S(1)} pad(f32[16,2,16]{1,2,0:T(8,128)} %pad_add_fusion, f32[]{:T(128)} %constant.7.clone.1), padding=0_0_0x1_0_1x0_0_0 | pad | bytes 6148 | tf_op jit(solution)/shard_map/pad | solution.py:63
  246.0 1.7 pad_maximum_fusion
  247.7 6.2 %pad.46 = f32[16,4,16]{1,2,0:T(8,128)S(1)} pad(f32[16,2,16]{1,2,0:T(8,128)} %pad_maximum_fusion, f32[]{:T(128)} %constant.7.clone.1), padding=0_0_0x0_1_1x0_0_0 | pad | bytes 6148 | tf_op jit(solution)/shard_map/pad | solution.py:63
  255.7 1.2 pad.48
  256.9 6.3 %pad.49 = f32[16,8,16]{1,2,0:T(8,128)S(1)} pad(f32[16,4,16]{1,2,0:T(8,128)} %add.156, f32[]{:T(128)} %constant.7.clone.1), padding=0_0_0x1_0_1x0_0_0 | pad | bytes 12292 | tf_op jit(solution)/shard_map/pad | solution.py:63
  264.3 1.3 pad.50
  265.7 1.4 pad.51
  268.2 1.6 pad.52
  269.8 1.6 pad.53
  272.6 2.1 pad.54
  274.7 2.2 pad.55
  276.9 3.2 pad.95
  280.1 3.2 pad.57
  284.3 3.2 pad.56
  288.9 15.5 %gather_fusion = f32[4096,16]{1,0:T(8,128)} fusion(f32[16,64]{0,1:T(8,128)S(1)} %bitcast.53, s32[4096]{0:T(1024)} %broadcast_clamp_fusion), kind=kCustom, calls=%fused_computation | custom fusion | bytes 540672 | tf_op jit(solution)/shard_map/gather | solution.py:57
  304.3 2.3 copy.90
  306.7 1.1 fusion.9
  307.8 1.1 convolution_add_fusion.1
  309.0 2.0 convolution_add_fusion
  311.0 1.4 copy.96
  312.4 1.1 add.169
  313.5 1.4 copy_add_fusion
  314.8 12.7 %all_to_all.29 = f32[16,8,1024]{2,0,1:T(8,128)S(1)} all-to-all(f32[16,8,1024]{2,0,1:T(8,128)S(1)} %copy_add_fusion), channel_id=1, replica_groups=mesh['ctx'=8,'mp'=32] {'ctx'}, dimensions={1} | all-to-all | bytes 1048576 | tf_op jit(solution)/shard_map/all_to_all | solution.py:117
  327.7 6.9 %convert_bitcast_fusion = bf16[4096,1024]{0,1:T(8,128)(2,1)} fusion(bf16[128,1024]{1,0:T(8,128)(2,1)S(1)} %fusion.8, bf16[128,4096]{1,0:T(8,128)(2,1)} %all-gather.9.cloned.1.call-done), kind=kOutput, calls=%fused_computation.1 | convolution fusion | flops 1077936128 | bytes 9699328 | tf_op jit(solution)/shard_map/dot_general | solution.py:123
  334.6 11.6 %copy.103 = bf16[4096,1024]{1,0:T(8,128)(2,1)} copy(bf16[4096,1024]{0,1:T(8,128)(2,1)} %convert_bitcast_fusion) | data formatting | bytes 16777216
  346.2 32.5 %all_gather.23 = f32[128,16]{1,0:T(8,128)S(1)} all-gather(f32[16,16]{1,0:T(8,128)S(1)} %get-tuple-element.20), channel_id=1, replica_groups=mesh['ctx'=8,'mp'=32] {'ctx'}, dimensions={0}, use_global_device_ids=true | all-gather | bytes 9216 | tf_op jit(solution)/shard_map/all_gather | solution.py:118
  379.3 93.1 %reduce-scatter.4.cloned.1.call-done = bf16[128,1024]{1,0:T(8,128)(2,1)} async-done(((bf16[4096,1024]{1,0:T(8,128)(2,1)}), bf16[128,1024]{1,0:T(8,128)(2,1)}) %reduce-scatter.4.cloned.1.call-update) | async-done | bytes 262160
  472.5 1.1 copy.104
  (109 shorter events, 31.1 us)
Async XLA Ops:
  7.2 182.0 %copy-start = (f32[128,16]{0,1:T(8,128)S(1)}, f32[128,16]{0,1:T(8,128)}, u32[]{:S(2)}) copy-start(f32[128,16]{0,1:T(8,128)} %param.19) | copy-start | bytes 24580
  7.2 41.1 %copy-start.1 = (bf16[1024,128]{1,0:T(8,128)(2,1)S(1)}, bf16[1024,128]{1,0:T(8,128)(2,1)}, u32[]{:S(2)}) copy-start(bf16[1024,128]{1,0:T(8,128)(2,1)} %param.13) | copy-start | bytes 786436
  7.2 41.1 %copy-start.13 = (f32[128]{0:T(128)S(1)}, f32[128]{0:T(128)}, u32[]{:S(2)}) copy-start(f32[128]{0:T(128)} %param.14) | copy-start | bytes 1540
  7.2 42.8 %copy-start.11 = (f32[3,3,128]{2,1,0:T(4,128)S(1)}, f32[3,3,128]{2,1,0:T(4,128)}, u32[]{:S(2)}) copy-start(f32[3,3,128]{2,1,0:T(4,128)} %param.17) | copy-start | bytes 13828
  7.2 42.8 %copy-start.9 = (f32[128,16]{0,1:T(8,128)S(1)}, f32[128,16]{0,1:T(8,128)}, u32[]{:S(2)}) copy-start(f32[128,16]{0,1:T(8,128)} %param.21) | copy-start | bytes 24580
  7.2 42.8 %copy-start.10 = (f32[128,16]{0,1:T(8,128)S(1)}, f32[128,16]{0,1:T(8,128)}, u32[]{:S(2)}) copy-start(f32[128,16]{0,1:T(8,128)} %param.18) | copy-start | bytes 24580
  7.2 77.6 %all-gather.7.cloned.1.call-start = ((), (), s32[]{:S(2)}) async-start(), calls=%async_computation.4 | async-start | bytes 3538944 | tf_op jit(solution)/shard_map/all_gather | solution.py:91
  9.3 168.1 %all-gather.5.cloned.1.call-start = ((), (), s32[]{:S(2)}) async-start(), calls=%async_computation.3 | async-start | bytes 8650752 | tf_op jit(solution)/shard_map/all_gather | solution.py:94
  49.2 278.4 %all-gather.9.cloned.1.call-start = ((), (), s32[]{:S(2)}) async-start(), calls=%async_computation.5 | async-start | bytes 1179648 | tf_op jit(solution)/shard_map/all_gather | solution.py:120
  50.2 134.9 %copy-start.6 = (f32[16,16]{1,0:T(8,128)}, f32[16,16]{1,0:T(8,128)S(1)}, u32[]{:S(2)}) copy-start(f32[16,16]{1,0:T(8,128)S(1)} %copy.106) | copy-start | bytes 3076
  50.8 168.3 %copy-start.4 = (f32[16,16]{1,0:T(8,128)}, f32[16,16]{1,0:T(8,128)S(1)}, u32[]{:S(2)}) copy-start(f32[16,16]{1,0:T(8,128)S(1)} %get-tuple-element.27) | copy-start | bytes 3076
  50.8 172.8 %copy-start.5 = (f32[16,16]{1,0:T(8,128)}, f32[16,16]{1,0:T(8,128)S(1)}, u32[]{:S(2)}) copy-start(f32[16,16]{1,0:T(8,128)S(1)} %get-tuple-element.28) | copy-start | bytes 3076
  177.4 11.9 %copy-start.12 = (bf16[3,128,2]{1,2,0:T(2,128)(2,1)S(1)}, bf16[3,128,2]{1,2,0:T(2,128)(2,1)}, u32[]{:S(2)}) copy-start(bf16[3,128,2]{1,2,0:T(2,128)(2,1)} %param.16) | copy-start | bytes 4612
  185.2 9.4 %collective-permute-start = (bf16[3,128,2]{2,1,0:T(8,128)(2,1)S(1)}, bf16[3,128,2]{2,1,0:T(8,128)(2,1)S(1)}, u32[]{:S(2)}, u32[]{:S(2)}) collective-permute-start(bf16[3,128,2]{2,1,0:T(8,128)(2,1)S(1)} %slice.240), channel_id=1, source_target_pairs={{0,32},{32,64},{64,96},{96,128},{128,160},{160,192},{192,224},{1,3... | collective-permute-start | bytes 4616 | tf_op jit(solution)/shard_map/ppermute | solution.py:14
  196.2 8.0 %copy-start.16 = (f32[128]{0:T(128)S(1)}, f32[128]{0:T(128)}, u32[]{:S(2)}) copy-start(f32[128]{0:T(128)} %param.20) | copy-start | bytes 1540
  196.2 11.1 %copy-start.7 = (s32[4096]{0:T(1024)S(1)}, s32[4096]{0:T(1024)}, u32[]{:S(2)}) copy-start(s32[4096]{0:T(1024)} %constant.70) | copy-start | bytes 49156
  197.0 13.0 %all-to-all-start = ((bf16[8,16,1024]{2,1,0:T(8,128)(2,1)}), bf16[8,16,1024]{2,1,0:T(8,128)(2,1)S(1)}, u32[]{:S(2)}, u32[]{:S(2)}) async-start(bf16[8,16,1024]{2,1,0:T(8,128)(2,1)} %bitcast.7), calls=%async_computation | async-start | bytes 524288 | tf_op jit(solution)/shard_map/all_to_all | solution.py:109
  203.6 268.9 %reduce-scatter.4.cloned.1.call-start = ((), (), s32[]{:S(2)}) async-start(), calls=%async_computation.6 | async-start | bytes 8650752
  268.1 15.3 %copy-start.2 = (f32[16,63,16]{1,2,0:T(8,128)S(1)}, f32[16,63,16]{1,2,0:T(8,128)}, u32[]{:S(2)}) copy-start(f32[16,63,16]{1,2,0:T(8,128)} %slice.235) | copy-start | bytes 193540
  304.3 2.4 copy-start.8
  306.7 2.3 copy-start.3
  306.7 2.3 copy-start.15
  311.0 2.5 copy-start.14
Sparse Core Ops, SparseCore 0:
  10.5 74.2 all-gather.6
  87.2 90.1 all-gather.4
  179.9 49.9 all-gather.8
  346.3 126.1 reduce-scatter.3
